TPU v7x, 32 devices: a whole 2x2x4 slice. The times are simulated.
32 devices in a mesh: dp: 8 (over y, x, core), seq: 4 (over z).
Axes of the slice: x: 2, y: 2, z: 4, core: 2. Of those that a mesh axis runs over, the one named last changes fastest.
Arguments:
- inputs: bfloat16 [8, 1024, 768], P('dp', 'seq'), may hold values from -6 to 6
- d_out: bfloat16 [8, 1024, 768], P('dp', 'seq'), may hold values from -6 to 6
- segments: int32 [8, 1024], P('dp'), may hold values from 0 to 1023, as said below
- buckets: int32 [2048], replicated, may hold values from 0 to 31
- w_query: bfloat16 [768, 768], P(('dp', 'seq')), may hold values from -0.21875 to 0.21875
- w_key: bfloat16 [768, 768], P(('dp', 'seq')), may hold values from -0.21875 to 0.21875
- w_value: bfloat16 [768, 768], P(('dp', 'seq')), may hold values from -0.21875 to 0.21875
- w_out: bfloat16 [768, 768], P(('dp', 'seq')), may hold values from -1.75 to 1.75
- w_gate: bfloat16 [768, 2048], P(('dp', 'seq')), may hold values from -0.21875 to 0.21875
- w_up: bfloat16 [768, 2048], P(('dp', 'seq')), may hold values from -0.21875 to 0.21875
- w_down: bfloat16 [2048, 768], P(('dp', 'seq')), may hold values from -0.1875 to 0.1875
- gain_attn: float32 [768], replicated, may hold values from 0.1 to 1.9
- gain_ffn: float32 [768], replicated, may hold values from 0.1 to 1.9
- bias_table: float32 [32, 12], replicated, may hold values from -4 to 4
Outputs:
- output: bfloat16 [8, 1024, 768], P('dp', 'seq')
- d_inputs: float32 [8, 1024, 768], P('dp', 'seq')
- grad_query: float32 [768, 768], P(('dp', 'seq'))
- grad_key: float32 [768, 768], P(('dp', 'seq'))
- grad_value: float32 [768, 768], P(('dp', 'seq'))
- grad_out: float32 [768, 768], P(('dp', 'seq'))
- grad_gate: float32 [768, 2048], P(('dp', 'seq'))
- grad_up: float32 [768, 2048], P(('dp', 'seq'))
- grad_down: float32 [2048, 768], P(('dp', 'seq'))
- grad_gain_attn: float32 [768], replicated
- grad_gain_ffn: float32 [768], replicated
- grad_table: float32 [32, 12], replicated
Inputs may be any that keep to these rules, and one draw needn't show every extreme that they name: `segments`: each row's label is the index of the last row of its document within the sequence; labels never fall along a sequence, and rows share a document exactly when they share a label.
All inputs are finite; a program needn't handle non-finite values.
Results may differ from a plain program's by a relative error of at most 0.015.
Values may be sent and summed in bfloat16 or wider, within the bound.
No kernel may reach another device: no remote copies, remote signals or barrier semaphores. Data moves between devices by JAX's collectives and lax.ppermute only.
A program may use at most 192 MiB of HBM per device.

v0:
```python
import jax
import jax.numpy as jnp
from jax import lax
from jax.sharding import PartitionSpec as P

EPS = 1e-06
MASKED = -1000000000.0
HIGHEST = lax.Precision.HIGHEST


def norm_rows(values, gain):
    return values * lax.rsqrt(jnp.mean(values * values, axis=-1, keepdims=True) + EPS) * gain


def geglu(gate_act, up_act):
    return jax.nn.gelu(gate_act, approximate=True) * up_act


def matmul(left, right):
    return jnp.dot(left, right, preferred_element_type=jnp.float32)


def left_matmul(left, right):
    return lax.dot_general(
        left, right, (((0,), (0,)), ((), ())), preferred_element_type=jnp.float32
    )


def right_matmul(left, right):
    return lax.dot_general(
        left, right, (((1,), (1,)), ((), ())), preferred_element_type=jnp.float32
    )


def shifted_bias(per_dist, query_count, key_count):
    head_count, width = per_dist.shape
    flipped = per_dist[:, ::-1]
    tiled = jnp.tile(flipped, (1, query_count + 1))[:, : query_count * (width + 1)]
    rows = tiled.reshape(head_count, query_count, width + 1)[:, :, :key_count]
    return rows[:, :, ::-1]


def diagonal_sums(scores):
    head_count, row_count, col_count = scores.shape
    row_width = row_count + col_count
    padded = jnp.concatenate(
        [jnp.zeros((head_count, row_count, row_count), scores.dtype), scores], axis=2
    )
    flat_rows = jnp.concatenate(
        [
            padded.reshape(head_count, row_count * row_width),
            jnp.zeros((head_count, row_count), scores.dtype),
        ],
        axis=1,
    )
    skewed = flat_rows.reshape(head_count, row_count, row_width + 1)
    return jnp.sum(skewed, axis=1)[:, 1:row_width]


def block_parts(
    queries,
    key_heads,
    value_heads,
    seg_query,
    seg_all,
    buckets,
    table,
    first_row,
    blk_index,
    key_block,
):
    query_count = queries.shape[0]
    seq_len = key_heads.shape[0]
    scale = queries.shape[-1] ** (-0.5)
    key_start = blk_index * key_block
    key_blk = lax.dynamic_slice_in_dim(key_heads, key_start, key_block)
    value_blk = lax.dynamic_slice_in_dim(value_heads, key_start, key_block)
    seg_keys = lax.dynamic_slice_in_dim(seg_all, key_start, key_block)
    dist_base = key_start - first_row - query_count + 1 + seq_len
    window = lax.dynamic_slice_in_dim(buckets, dist_base, query_count + key_block - 1)
    onehot = (window[:, None] == jnp.arange(table.shape[0], dtype=jnp.int32)[None, :]).astype(
        jnp.float32
    )
    per_dist = jnp.dot(onehot, table, precision=HIGHEST).T
    bias_blk = shifted_bias(per_dist, query_count, key_block)
    raw_scores = (
        jnp.einsum("qhd,khd->hqk", queries, key_blk, preferred_element_type=jnp.float32) * scale
        + bias_blk
    )
    same_doc = (seg_query[:, None] == seg_keys[None, :])[None]
    weights_exp = jnp.exp(jnp.where(same_doc, raw_scores, MASKED))
    return (key_blk, value_blk, onehot, weights_exp)


def local(
    inputs,
    d_out,
    segments,
    buckets,
    w_query,
    w_key,
    w_value,
    w_out,
    w_gate,
    w_up,
    w_down,
    gain_attn,
    gain_ffn,
    bias_table,
):
    seq_count, row_count, model_width = inputs.shape
    seq_len = segments.shape[1]
    head_count = bias_table.shape[1]
    head_dim = model_width // head_count
    key_block = min(512, seq_len)
    block_count = seq_len // key_block
    token_count = seq_count * row_count
    scale = head_dim ** (-0.5)
    first_row = lax.axis_index("seq") * row_count
    blk_ids = jnp.arange(block_count, dtype=jnp.int32)
    gathered = (
        lax.all_gather(w_query, ("dp", "seq"), axis=0, tiled=True),
        lax.all_gather(w_key, ("dp", "seq"), axis=0, tiled=True),
        lax.all_gather(w_value, ("dp", "seq"), axis=0, tiled=True),
        lax.all_gather(w_out, ("dp", "seq"), axis=0, tiled=True),
        lax.all_gather(w_gate, ("dp", "seq"), axis=0, tiled=True),
        lax.all_gather(w_up, ("dp", "seq"), axis=0, tiled=True),
        lax.all_gather(w_down, ("dp", "seq"), axis=0, tiled=True),
    )
    full_query, full_key, full_value, full_out, full_gate, full_up, full_down = gathered
    flat_in = inputs.reshape(token_count, model_width).astype(jnp.float32)
    normed = norm_rows(flat_in, gain_attn).astype(jnp.bfloat16)
    queries = matmul(normed, full_query).astype(jnp.bfloat16)
    key_rows = (
        matmul(normed, full_key).astype(jnp.bfloat16).reshape(seq_count, row_count, model_width)
    )
    value_rows = (
        matmul(normed, full_value).astype(jnp.bfloat16).reshape(seq_count, row_count, model_width)
    )
    key_all, value_all = (
        lax.all_gather(key_rows, "seq", axis=1, tiled=True),
        lax.all_gather(value_rows, "seq", axis=1, tiled=True),
    )
    query_heads = queries.reshape(seq_count, row_count, head_count, head_dim)
    key_heads = key_all.reshape(seq_count, seq_len, head_count, head_dim)
    value_heads = value_all.reshape(seq_count, seq_len, head_count, head_dim)
    seg_queries = lax.dynamic_slice_in_dim(segments, first_row, row_count, axis=1)

    def attend(packed):
        query_one, key_one, value_one, seg_query, seg_all = packed

        def step(state_in, blk_index):
            totals, summed = state_in
            _, value_blk, _, weights_exp = block_parts(
                query_one,
                key_one,
                value_one,
                seg_query,
                seg_all,
                buckets,
                bias_table,
                first_row,
                blk_index,
                key_block,
            )
            summed = summed + jnp.einsum(
                "hqk,khd->qhd",
                weights_exp.astype(jnp.bfloat16),
                value_blk,
                preferred_element_type=jnp.float32,
            )
            totals = totals + jnp.sum(weights_exp, axis=-1)
            return ((totals, summed), None)

        start_state = (
            jnp.zeros((head_count, row_count), jnp.float32),
            jnp.zeros((row_count, head_count, head_dim), jnp.float32),
        )
        (totals, summed), _ = lax.scan(step, start_state, blk_ids)
        return (summed / jnp.transpose(totals)[:, :, None], totals)

    attn_f32, totals_all = lax.map(
        attend, (query_heads, key_heads, value_heads, seg_queries, segments)
    )
    attn_rows = attn_f32.reshape(token_count, model_width).astype(jnp.bfloat16)
    mixed_rows = flat_in + matmul(attn_rows, full_out)
    normed_two = norm_rows(mixed_rows, gain_ffn).astype(jnp.bfloat16)
    gate_act = matmul(normed_two, full_gate)
    up_act = matmul(normed_two, full_up)
    hidden = geglu(gate_act, up_act).astype(jnp.bfloat16)
    result = mixed_rows + matmul(hidden, full_down)
    output = result.astype(jnp.bfloat16).reshape(seq_count, row_count, model_width)
    back_weights = (
        lax.all_gather(w_query, ("dp", "seq"), axis=0, tiled=True),
        lax.all_gather(w_key, ("dp", "seq"), axis=0, tiled=True),
        lax.all_gather(w_value, ("dp", "seq"), axis=0, tiled=True),
        lax.all_gather(w_out, ("dp", "seq"), axis=0, tiled=True),
        lax.all_gather(w_gate, ("dp", "seq"), axis=0, tiled=True),
        lax.all_gather(w_up, ("dp", "seq"), axis=0, tiled=True),
        lax.all_gather(w_down, ("dp", "seq"), axis=0, tiled=True),
    )
    back_query, back_key, back_value, back_out, back_gate, back_up, back_down = back_weights
    d_res = d_out.reshape(token_count, model_width)
    grad_down = left_matmul(hidden, d_res)
    d_hidden = right_matmul(d_res, back_down)
    _, geglu_back = jax.vjp(geglu, gate_act, up_act)
    d_gate, d_up = geglu_back(d_hidden)
    d_gate = d_gate.astype(jnp.bfloat16)
    d_up = d_up.astype(jnp.bfloat16)
    grad_gate = left_matmul(normed_two, d_gate)
    grad_up = left_matmul(normed_two, d_up)
    d_normed_two = right_matmul(d_gate, back_gate) + right_matmul(d_up, back_up)
    _, norm_two_back = jax.vjp(norm_rows, mixed_rows, gain_ffn)
    d_mixed_norm, grad_gain_ffn = norm_two_back(d_normed_two)
    d_mixed = d_res.astype(jnp.float32) + d_mixed_norm
    d_branch = d_mixed.astype(jnp.bfloat16)
    grad_out = left_matmul(attn_rows, d_branch)
    d_attn = right_matmul(d_branch, back_out).reshape(seq_count, row_count, head_count, head_dim)
    totals_rows = jnp.transpose(totals_all, (0, 2, 1))
    d_unnorm_all = (d_attn / totals_rows[:, :, :, None]).astype(jnp.bfloat16)
    correction_all = -jnp.sum(d_attn * attn_f32, axis=-1) / totals_rows

    def attend_back(packed):
        query_one, key_one, value_one, seg_query, seg_all, d_unnorm, corr_rows = packed
        correction = jnp.transpose(corr_rows)

        def step(state_in, blk_index):
            d_query, d_table = state_in
            key_blk, value_blk, onehot, weights_exp = block_parts(
                query_one,
                key_one,
                value_one,
                seg_query,
                seg_all,
                buckets,
                bias_table,
                first_row,
                blk_index,
                key_block,
            )
            d_prob = jnp.einsum(
                "qhd,khd->hqk", d_unnorm, value_blk, preferred_element_type=jnp.float32
            )
            d_raw = (weights_exp * (d_prob + correction[:, :, None])).astype(jnp.bfloat16)
            d_query = (
                d_query
                + jnp.einsum("hqk,khd->qhd", d_raw, key_blk, preferred_element_type=jnp.float32)
                * scale
            )
            d_table = d_table + jnp.dot(
                diagonal_sums(d_raw.astype(jnp.float32)), onehot, precision=HIGHEST
            )
            d_key = (
                jnp.einsum("hqk,qhd->khd", d_raw, query_one, preferred_element_type=jnp.float32)
                * scale
            )
            d_value = jnp.einsum(
                "hqk,qhd->khd",
                weights_exp.astype(jnp.bfloat16),
                d_unnorm,
                preferred_element_type=jnp.float32,
            )
            return ((d_query, d_table), (d_key, d_value))

        start_state = (
            jnp.zeros((row_count, head_count, head_dim), jnp.float32),
            jnp.zeros((head_count, bias_table.shape[0]), jnp.float32),
        )
        (d_query, d_table), key_parts = lax.scan(step, start_state, blk_ids)
        d_key, d_value = key_parts
        return (
            d_query,
            d_table,
            d_key.reshape(seq_len, model_width),
            d_value.reshape(seq_len, model_width),
        )

    back_inputs = (
        query_heads,
        key_heads,
        value_heads,
        seg_queries,
        segments,
        d_unnorm_all,
        correction_all,
    )
    d_query_all, d_table_all, d_key_all, d_value_all = lax.map(attend_back, back_inputs)
    d_key_own, d_value_own = (
        lax.psum_scatter(
            d_key_all.astype(jnp.bfloat16), "seq", scatter_dimension=1, tiled=True
        ).astype(jnp.float32),
        lax.psum_scatter(
            d_value_all.astype(jnp.bfloat16), "seq", scatter_dimension=1, tiled=True
        ).astype(jnp.float32),
    )
    d_query_b = d_query_all.reshape(token_count, model_width).astype(jnp.bfloat16)
    d_key_b = d_key_own.reshape(token_count, model_width).astype(jnp.bfloat16)
    d_value_b = d_value_own.reshape(token_count, model_width).astype(jnp.bfloat16)
    grad_query = left_matmul(normed, d_query_b)
    grad_key = left_matmul(normed, d_key_b)
    grad_value = left_matmul(normed, d_value_b)
    d_normed = (
        right_matmul(d_query_b, back_query)
        + right_matmul(d_key_b, back_key)
        + right_matmul(d_value_b, back_value)
    )
    _, norm_one_back = jax.vjp(norm_rows, flat_in, gain_attn)
    d_in_norm, grad_gain_attn = norm_one_back(d_normed)
    d_inputs = (d_mixed + d_in_norm).reshape(seq_count, row_count, model_width)
    owned = (
        lax.psum_scatter(grad_query, ("dp", "seq"), scatter_dimension=0, tiled=True),
        lax.psum_scatter(grad_key, ("dp", "seq"), scatter_dimension=0, tiled=True),
        lax.psum_scatter(grad_value, ("dp", "seq"), scatter_dimension=0, tiled=True),
        lax.psum_scatter(grad_out, ("dp", "seq"), scatter_dimension=0, tiled=True),
        lax.psum_scatter(grad_gate, ("dp", "seq"), scatter_dimension=0, tiled=True),
        lax.psum_scatter(grad_up, ("dp", "seq"), scatter_dimension=0, tiled=True),
        lax.psum_scatter(grad_down, ("dp", "seq"), scatter_dimension=0, tiled=True),
    )
    table_local = jnp.transpose(jnp.sum(d_table_all, axis=0))
    gain_one, gain_two, table_grad = lax.psum(
        (grad_gain_attn, grad_gain_ffn, table_local), ("dp", "seq")
    )
    return (
        output,
        d_inputs,
        owned[0],
        owned[1],
        owned[2],
        owned[3],
        owned[4],
        owned[5],
        owned[6],
        gain_one,
        gain_two,
        table_grad,
    )


def solution(mesh):
    return jax.shard_map(
        local,
        mesh=mesh,
        in_specs=(
            P("dp", "seq", None),
            P("dp", "seq", None),
            P("dp", None),
            P(),
            P(("dp", "seq"), None),
            P(("dp", "seq"), None),
            P(("dp", "seq"), None),
            P(("dp", "seq"), None),
            P(("dp", "seq"), None),
            P(("dp", "seq"), None),
            P(("dp", "seq"), None),
            P(),
            P(),
            P(),
        ),
        out_specs=(
            P("dp", "seq", None),
            P("dp", "seq", None),
            P(("dp", "seq"), None),
            P(("dp", "seq"), None),
            P(("dp", "seq"), None),
            P(("dp", "seq"), None),
            P(("dp", "seq"), None),
            P(("dp", "seq"), None),
            P(("dp", "seq"), None),
            P(),
            P(),
            P(),
        ),
        check_vma=False,
    )
```

profile of v0, /device:TPU:0, one launch (start us, length us, event | category | flops | bytes accessed | tf_op | source)
XLA Modules:
  0.0 1757.2 jit_solution(12982344528251555989)
XLA Ops:
  10.7 57.0 %all-gather.16.cloned.1.call-done = bf16[768,768]{1,0:T(8,128)(2,1)} async-done(((bf16[24,768]{1,0:T(8,128)(2,1)}), bf16[768,768]{1,0:T(8,128)(2,1)}) %all-gather.16.cloned.1.call-update) | async-done | bytes 1179664 | tf_op jit(solution)/shard_map/all_gather | solution.py:124
  70.4 53.1 %all-gather.12.cloned.1.call-done = bf16[768,768]{1,0:T(8,128)(2,1)} async-done(((bf16[24,768]{1,0:T(8,128)(2,1)}), bf16[768,768]{1,0:T(8,128)(2,1)}) %all-gather.12.cloned.1.call-update) | async-done | bytes 1179664 | tf_op jit(solution)/shard_map/all_gather | solution.py:123
  130.3 49.1 %all-gather.14.cloned.1.call-done = bf16[768,768]{1,0:T(8,128)(2,1)} async-done(((bf16[24,768]{1,0:T(8,128)(2,1)}), bf16[768,768]{1,0:T(8,128)(2,1)}) %all-gather.14.cloned.1.call-update) | async-done | bytes 1179664 | tf_op jit(solution)/shard_map/all_gather | solution.py:122
  181.4 35.5 %all-gather.28.cloned.1.call-done = bf16[1024,768]{1,0:T(8,128)(2,1)} async-done(((bf16[256,768]{1,0:T(8,128)(2,1)}), bf16[1024,768]{1,0:T(8,128)(2,1)}) %all-gather.28.cloned.1.call-update) | async-done | bytes 1572880 | tf_op jit(solution)/shard_map/all_gather | solution.py:142
  218.6 36.3 %all-gather.26.cloned.1.call-done = bf16[1024,768]{1,0:T(8,128)(2,1)} async-done(((bf16[256,768]{1,0:T(8,128)(2,1)}), bf16[1024,768]{1,0:T(8,128)(2,1)}) %all-gather.26.cloned.1.call-update) | async-done | bytes 1572880 | tf_op jit(solution)/shard_map/all_gather | solution.py:141
  257.1 241.5 %while.60 = (s32[]{:T(128)}, f32[12,256]{1,0:T(8,128)S(1)}, f32[256,12,64]{0,2,1:T(8,128)}, s32[256]{0:T(256)}, s32[2]{0:T(128)}, /*index=5*/s32[1024]{0:T(1024)...) while((s32[]{:T(128)}, f32[12,256]{1,0:T(8,128)S(1)}, ...), condition=%wide.region_3.4_spmd.clone, body=%wide.region_1.3_spmd.clone.sunk | while | flops 414603776 | bytes 133137936 | solution.py:179
  273.0 14.2 tile.39
  322.9 48.3 %rev.42 = f32[12,256,512]{1,2,0:T(8,128)} reverse(f32[12,256,512]{1,2,0:T(8,128)} %copy.69), dimensions={2} | reverse | bytes 12582912 | tf_op jit(solution)/shard_map/while/body/eval_jaxpr/while/body/eval_jaxpr/rev | solution.py:40
  443.5 48.3 %rev.42 = f32[12,256,512]{1,2,0:T(8,128)} reverse(f32[12,256,512]{1,2,0:T(8,128)} %copy.69), dimensions={2} | reverse | bytes 12582912 | tf_op jit(solution)/shard_map/while/body/eval_jaxpr/while/body/eval_jaxpr/rev | solution.py:40
  528.6 368.2 %while.61 = (s32[]{:T(128)}, f32[256,12,64]{0,2,1:T(8,128)}, f32[12,32]{1,0:T(8,128)}, bf16[2,512,12,64]{1,3,2,0:T(8,128)(2,1)}, bf16[2,512,12,64]{1,3,2,0:T(8,1...) while((s32[]{:T(128)}, f32[256,12,64]{0,2,1:T(8,128)}, ...), condition=%wide.region_9.10_spmd.clone, body=%wide.region_7.9_spmd.clone.sunk | while | flops 1030591232 | bytes 274231168 | solution.py:269
  613.7 48.3 %rev.43 = f32[12,256,512]{1,2,0:T(8,128)} reverse(f32[12,256,512]{1,2,0:T(8,128)} %copy.71), dimensions={2} | reverse | bytes 12582912 | tf_op jit(solution)/shard_map/while/body/eval_jaxpr/while/body/eval_jaxpr/rev | solution.py:40
  689.4 20.8 %reshape.329 = f32[12,256,769]{2,1,0:T(8,128)} reshape(f32[12,196864]{1,0:T(8,128)} %pad_convert_fusion.2) | data formatting | bytes 18898944 | tf_op jit(solution)/shard_map/while/body/eval_jaxpr/while/body/eval_jaxpr/reshape | solution.py:56
  783.6 48.3 %rev.43 = f32[12,256,512]{1,2,0:T(8,128)} reverse(f32[12,256,512]{1,2,0:T(8,128)} %copy.71), dimensions={2} | reverse | bytes 12582912 | tf_op jit(solution)/shard_map/while/body/eval_jaxpr/while/body/eval_jaxpr/rev | solution.py:40
  859.5 20.8 %reshape.329 = f32[12,256,769]{2,1,0:T(8,128)} reshape(f32[12,196864]{1,0:T(8,128)} %pad_convert_fusion.2) | data formatting | bytes 18898944 | tf_op jit(solution)/shard_map/while/body/eval_jaxpr/while/body/eval_jaxpr/reshape | solution.py:56
  913.2 23.5 %reduce-scatter.12.cloned.1.call-done = bf16[1,256,768]{1,2,0:T(8,128)(2,1)} async-done(((bf16[1,1024,768]{1,2,0:T(8,128)(2,1)}), bf16[1,256,768]{1,2,0:T(8,128)(2,1)}) %reduce-scatter.12.cloned.1.call-update) | async-done | bytes 393232 | tf_op jit(solution)/shard_map/reduce_scatter | solution.py:292
  939.9 33.5 %reduce-scatter.10.cloned.1.call-done = bf16[1,256,768]{1,2,0:T(8,128)(2,1)} async-done(((bf16[1,1024,768]{1,2,0:T(8,128)(2,1)}), bf16[1,256,768]{1,2,0:T(8,128)(2,1)}) %reduce-scatter.10.cloned.1.call-update) | async-done | bytes 393232 | tf_op jit(solution)/shard_map/reduce_scatter | solution.py:289
  998.0 39.6 %all-reduce.2 = (f32[768]{0:T(1024)}, f32[768]{0:T(1024)}, f32[32,12]{0,1:T(8,128)}) all-reduce(f32[768]{0:T(1024)S(1)} %get-tuple-element.776, f32[768]{0:T(1024)S(1)} %copy-done.44, f32[32,12]{0,1:T(8,128)S(1)} %bitcast.253), channel_id=1, replica_groups=mesh['dp'=8,'seq'=4] {'dp','seq'}, use_global_device_ids=true, to_apply=%region_21.22 | all-reduce | flops 1920 | bytes 15360 | tf_op jit(solution)/shard_map/psum | solution.py:320
  1038.7 38.5 %reduce-scatter.20.cloned.1.call-done = f32[24,768]{1,0:T(8,128)} async-done(((f32[768,768]{1,0:T(8,128)}), f32[24,768]{1,0:T(8,128)}) %reduce-scatter.20.cloned.1.call-update) | async-done | bytes 73744 | tf_op jit(solution)/shard_map/reduce_scatter | solution.py:314
  1077.2 104.8 %reduce-scatter.14.cloned.1.call-done = f32[24,768]{1,0:T(8,128)} async-done(((f32[768,768]{1,0:T(8,128)}), f32[24,768]{1,0:T(8,128)}) %reduce-scatter.14.cloned.1.call-update) | async-done | bytes 73744 | tf_op jit(solution)/shard_map/reduce_scatter | solution.py:311
  1181.9 103.8 %reduce-scatter.18.cloned.1.call-done = f32[24,768]{1,0:T(8,128)} async-done(((f32[768,768]{1,0:T(8,128)}), f32[24,768]{1,0:T(8,128)}) %reduce-scatter.18.cloned.1.call-update) | async-done | bytes 73744 | tf_op jit(solution)/shard_map/reduce_scatter | solution.py:313
  1285.8 104.6 %reduce-scatter.16.cloned.1.call-done = f32[24,768]{1,0:T(8,128)} async-done(((f32[768,768]{1,0:T(8,128)}), f32[24,768]{1,0:T(8,128)}) %reduce-scatter.16.cloned.1.call-update) | async-done | bytes 73744 | tf_op jit(solution)/shard_map/reduce_scatter | solution.py:312
  1390.3 119.4 %reduce-scatter.26.cloned.1.call-done = f32[64,768]{1,0:T(8,128)} async-done(((f32[2048,768]{1,0:T(8,128)}), f32[64,768]{1,0:T(8,128)}) %reduce-scatter.26.cloned.1.call-update) | async-done | bytes 196624 | tf_op jit(solution)/shard_map/reduce_scatter | solution.py:317
  1509.7 120.6 %reduce-scatter.24.cloned.1.call-done = f32[24,2048]{1,0:T(8,128)} async-done(((f32[768,2048]{1,0:T(8,128)}), f32[24,2048]{1,0:T(8,128)}) %reduce-scatter.24.cloned.1.call-update) | async-done | bytes 196624 | tf_op jit(solution)/shard_map/reduce_scatter | solution.py:316
  1630.3 119.9 %reduce-scatter.22.cloned.1.call-done = f32[24,2048]{1,0:T(8,128)} async-done(((f32[768,2048]{1,0:T(8,128)}), f32[24,2048]{1,0:T(8,128)}) %reduce-scatter.22.cloned.1.call-update) | async-done | bytes 196624 | tf_op jit(solution)/shard_map/reduce_scatter | solution.py:315
  (308 shorter events, 422.5 us)
Async XLA Ops:
  7.2 116.4 %copy-start.8 = (bf16[1,256,768]{2,1,0:T(8,128)(2,1)S(1)}, bf16[1,256,768]{2,1,0:T(8,128)(2,1)}, u32[]{:S(2)}) copy-start(bf16[1,256,768]{2,1,0:T(8,128)(2,1)} %param.18) | copy-start | bytes 1179652
  7.2 116.3 %copy-start.36 = (f32[768]{0:T(1024)S(1)}, f32[768]{0:T(1024)}, u32[]{:S(2)}) copy-start(f32[768]{0:T(1024)} %param.29) | copy-start | bytes 9220
  7.2 60.5 %all-gather.16.cloned.1.call-start = ((), (), s32[]{:S(2)}) async-start(), calls=%async_computation.11 | async-start | bytes 1216512 | tf_op jit(solution)/shard_map/all_gather | solution.py:124
  7.9 115.6 %all-gather.12.cloned.1.call-start = ((), (), s32[]{:S(2)}) async-start(), calls=%async_computation.9 | async-start | bytes 1216512 | tf_op jit(solution)/shard_map/all_gather | solution.py:123
  8.7 170.7 %all-gather.14.cloned.1.call-start = ((), (), s32[]{:S(2)}) async-start(), calls=%async_computation.10 | async-start | bytes 1216512 | tf_op jit(solution)/shard_map/all_gather | solution.py:122
  9.4 207.5 %all-gather.28.cloned.1.call-start = ((), (), s32[]{:S(2)}) async-start(), calls=%async_computation.26 | async-start | bytes 1966080 | tf_op jit(solution)/shard_map/all_gather | solution.py:142
  10.6 115.5 %copy-start.49 = (f32[256]{0:T(256)}, f32[256]{0:T(256)S(1)}, u32[]{:S(2)}) copy-start(f32[256]{0:T(256)S(1)} %fusion.50) | copy-start | bytes 3076
  10.6 168.8 %copy-start.42 = (f32[256]{0:T(256)}, f32[256]{0:T(256)S(1)}, u32[]{:S(2)}) copy-start(f32[256]{0:T(256)S(1)} %fusion.74) | copy-start | bytes 3076
  70.4 184.5 %all-gather.26.cloned.1.call-start = ((), (), s32[]{:S(2)}) async-start(), calls=%async_computation.25 | async-start | bytes 1966080 | tf_op jit(solution)/shard_map/all_gather | solution.py:141
  126.1 374.4 %all-gather.18.cloned.1.call-start = ((), (), s32[]{:S(2)}) async-start(), calls=%async_computation.12 | async-start | bytes 1216512 | tf_op jit(solution)/shard_map/all_gather | solution.py:125
  126.7 378.0 %all-gather.22.cloned.1.call-start = ((), (), s32[]{:S(2)}) async-start(), calls=%async_computation.14 | async-start | bytes 3244032 | tf_op jit(solution)/shard_map/all_gather | solution.py:127
  127.4 381.6 %all-gather.20.cloned.1.call-start = ((), (), s32[]{:S(2)}) async-start(), calls=%async_computation.13 | async-start | bytes 3244032 | tf_op jit(solution)/shard_map/all_gather | solution.py:126
  128.2 385.2 %all-gather.24.cloned.1.call-start = ((), (), s32[]{:S(2)}) async-start(), calls=%async_computation.15 | async-start | bytes 3244032 | tf_op jit(solution)/shard_map/all_gather | solution.py:128
  128.9 807.9 %reduce-scatter.12.cloned.1.call-start = ((), (), s32[]{:S(2)}) async-start(), calls=%async_computation.17 | async-start | bytes 1966080 | tf_op jit(solution)/shard_map/reduce_scatter | solution.py:292
  547.7 114.4 %copy-start.2 = (bf16[1024,12,64]{0,2,1:T(8,128)(2,1)}, bf16[1024,12,64]{0,2,1:T(8,128)(2,1)S(1)}, u32[]{:S(2)}) copy-start(bf16[1024,12,64]{0,2,1:T(8,128)(2,1)S(1)} %get-tuple-element.1132) | copy-start | bytes 4718596 | tf_op jit(solution)/shard_map/while/body/eval_jaxpr/while
  717.5 114.4 %copy-start.2 = (bf16[1024,12,64]{0,2,1:T(8,128)(2,1)}, bf16[1024,12,64]{0,2,1:T(8,128)(2,1)S(1)}, u32[]{:S(2)}) copy-start(bf16[1024,12,64]{0,2,1:T(8,128)(2,1)S(1)} %get-tuple-element.1132) | copy-start | bytes 4718596 | tf_op jit(solution)/shard_map/while/body/eval_jaxpr/while
  902.3 71.1 %reduce-scatter.10.cloned.1.call-start = ((), (), s32[]{:S(2)}) async-start(), calls=%async_computation.16 | async-start | bytes 1966080 | tf_op jit(solution)/shard_map/reduce_scatter | solution.py:289
  907.8 169.4 %reduce-scatter.20.cloned.1.call-start = ((), (), s32[]{:S(2)}) async-start(), calls=%async_computation.21 | async-start | bytes 2433024 | tf_op jit(solution)/shard_map/reduce_scatter | solution.py:314
  909.8 272.1 %reduce-scatter.14.cloned.1.call-start = ((), (), s32[]{:S(2)}) async-start(), calls=%async_computation.18 | async-start | bytes 2433024 | tf_op jit(solution)/shard_map/reduce_scatter | solution.py:311
  913.2 372.6 %reduce-scatter.18.cloned.1.call-start = ((), (), s32[]{:S(2)}) async-start(), calls=%async_computation.20 | async-start | bytes 2433024 | tf_op jit(solution)/shard_map/reduce_scatter | solution.py:313
  939.8 450.5 %reduce-scatter.16.cloned.1.call-start = ((), (), s32[]{:S(2)}) async-start(), calls=%async_computation.19 | async-start | bytes 2433024 | tf_op jit(solution)/shard_map/reduce_scatter | solution.py:312
  976.4 533.4 %reduce-scatter.26.cloned.1.call-start = ((), (), s32[]{:S(2)}) async-start(), calls=%async_computation.24 | async-start | bytes 6488064 | tf_op jit(solution)/shard_map/reduce_scatter | solution.py:317
  980.2 650.1 %reduce-scatter.24.cloned.1.call-start = ((), (), s32[]{:S(2)}) async-start(), calls=%async_computation.23 | async-start | bytes 6488064 | tf_op jit(solution)/shard_map/reduce_scatter | solution.py:316
  985.2 765.0 %reduce-scatter.22.cloned.1.call-start = ((), (), s32[]{:S(2)}) async-start(), calls=%async_computation.22 | async-start | bytes 6488064 | tf_op jit(solution)/shard_map/reduce_scatter | solution.py:315
  (63 other events, 395.3 us)
Sparse Core Ops, SparseCore 0:
  10.8 56.7 all-gather.15
  70.5 53.0 all-gather.11
  126.3 53.0 all-gather.13
  180.8 36.0 all-gather.27
  218.9 35.9 all-gather.25
  257.5 52.9 all-gather.17
  313.4 57.9 all-gather.21
  374.3 57.8 all-gather.19
  435.1 57.8 all-gather.23
  902.4 34.2 reduce-scatter.11
  939.1 34.2 reduce-scatter.9
  979.1 98.0 reduce-scatter.19
  1083.9 98.0 reduce-scatter.13
  1187.6 98.0 reduce-scatter.17
  1292.3 97.9 reduce-scatter.15
  1396.4 113.3 reduce-scatter.25
  1516.7 113.5 reduce-scatter.23
  1636.4 113.7 reduce-scatter.21
where the time goes:
time: 1780 us; the launch traced here: 1760 us
  waiting for transfers between devices  1000 us (56%)
  local copies, waits for them, and re-layouts  529 us (30%)
  matrix products  102 us (6%)
  blocking collectives  39.6 us (2%)
  other arithmetic  35 us (2%)
  loops' own time  31.6 us (2%)
    rev x4, local copies, waits for them, and re-layouts, shifted_bias(): return rows[:, :, ::-1]  193 us
    reduce_scatter x1, waiting for transfers between devices, local(): lax.psum_scatter(grad_up, ('dp', 'seq'), scatter_dimension=0, tiled=True)  121 us
    reduce_scatter x1, waiting for transfers between devices, local(): lax.psum_scatter(grad_gate, ('dp', 'seq'), scatter_dimension=0, tiled=True)  120 us
    reduce_scatter x1, waiting for transfers between devices, local(): lax.psum_scatter(grad_down, ('dp', 'seq'), scatter_dimension=0, tiled=True)  119 us
    while x82, local copies, waits for them, and re-layouts  113 us
    reduce_scatter x1, waiting for transfers between devices, local(): lax.psum_scatter(grad_query, ('dp', 'seq'), scatter_dimension=0, tiled=True)  105 us
    reduce_scatter x1, waiting for transfers between devices, local(): lax.psum_scatter(grad_key, ('dp', 'seq'), scatter_dimension=0, tiled=True)  105 us
    reduce_scatter x1, waiting for transfers between devices, local(): lax.psum_scatter(grad_value, ('dp', 'seq'), scatter_dimension=0, tiled=True)  104 us
  transfers between devices with their start and end apart: 18, of which 14 were waited for; matrix products, arithmetic and copies ran while one was open for 17% of the time, Pallas kernels for 0%

commit v1 on v0

--- a/solution.py
+++ b/solution.py
@@ -6,6 +6,28 @@
 EPS = 1e-06
 MASKED = -1000000000.0
 HIGHEST = lax.Precision.HIGHEST
+
+
+def laid_out(parts, dim):
+    lengths = list(parts.shape[1:])
+    lengths[dim] *= parts.shape[0]
+    return jnp.moveaxis(parts, 0, dim).reshape(lengths)
+
+
+def gather_around(x, axis, dim):
+    devices = lax.axis_size(axis)
+    pairs = [(i, (i + 1) % devices) for i in range(devices)]
+    back = [(b, a) for a, b in pairs]
+    lower, upper = ([], [])
+    for turn in range(devices - 1):
+        if turn % 2 == 0:
+            lower.append(lax.ppermute(lower[-1] if lower else x, axis, pairs))
+        else:
+            upper.append(lax.ppermute(upper[-1] if upper else x, axis, back))
+    blocks = jnp.stack([*lower[::-1], x, *upper])
+    shift = lax.axis_index(axis) - len(lower)
+    blocks = blocks[(jnp.arange(devices) - shift) % devices]
+    return laid_out(blocks, dim)
 
 
 def norm_rows(values, gain):
@@ -139,7 +161,7 @@
     )
     key_all, value_all = (
         lax.all_gather(key_rows, "seq", axis=1, tiled=True),
-        lax.all_gather(value_rows, "seq", axis=1, tiled=True),
+        gather_around(value_rows, "seq", 1),
     )
     query_heads = queries.reshape(seq_count, row_count, head_count, head_dim)
     key_heads = key_all.reshape(seq_count, seq_len, head_count, head_dim)

time: 1780 us -> 1730 us (0.972)
  waiting for transfers between devices: 1000 us -> 962 us
  loops' own time: 31.6 us -> 13.2 us
    all_gather x1 -> x0, waiting for transfers between devices: 35.5 us -> none  [local(): lax.all_gather(value_rows, 'seq', axis=1, tiled=True)]
    another operation x1, loops' own time: 29.9 us -> 11 us  [attend_back(): (d_query, d_table), key_parts = lax.scan(step, start_state, blk_ids)]
  transfers between devices with their start and end apart: 18 -> 20, of which waited for: 14 -> 14; matrix products, arithmetic and copies ran while one was open for 17% -> 18% of each run, Pallas kernels for 0% -> 0%
where the time goes in v1:
time: 1730 us; the launch traced here: 1700 us
  waiting for transfers between devices  962 us (56%)
  local copies, waits for them, and re-layouts  533 us (31%)
  matrix products  101 us (6%)
  blocking collectives  39.6 us (2%)
  other arithmetic  35.8 us (2%)
    rev x4, local copies, waits for them, and re-layouts, shifted_bias(): return rows[:, :, ::-1]  193 us
    reduce_scatter x1, waiting for transfers between devices, local(): lax.psum_scatter(grad_up, ('dp', 'seq'), scatter_dimension=0, tiled=True)  121 us
    reduce_scatter x1, waiting for transfers between devices, local(): lax.psum_scatter(grad_gate, ('dp', 'seq'), scatter_dimension=0, tiled=True)  120 us
    reduce_scatter x1, waiting for transfers between devices, local(): lax.psum_scatter(grad_down, ('dp', 'seq'), scatter_dimension=0, tiled=True)  119 us
    while x82, local copies, waits for them, and re-layouts  113 us
    reduce_scatter x1, waiting for transfers between devices, local(): lax.psum_scatter(grad_key, ('dp', 'seq'), scatter_dimension=0, tiled=True)  105 us
    reduce_scatter x1, waiting for transfers between devices, local(): lax.psum_scatter(grad_query, ('dp', 'seq'), scatter_dimension=0, tiled=True)  105 us
    reduce_scatter x1, waiting for transfers between devices, local(): lax.psum_scatter(grad_value, ('dp', 'seq'), scatter_dimension=0, tiled=True)  104 us
  transfers between devices with their start and end apart: 20, of which 14 were waited for; matrix products, arithmetic and copies ran while one was open for 18% of the time, Pallas kernels for 0%

profile of v1, /device:TPU:0, one launch (start us, length us, event | category | flops | bytes accessed | tf_op | source)
XLA Modules:
  0.0 1704.5 jit_solution(8295543324982151573)
XLA Ops:
  10.7 57.0 %all-gather.10.cloned.1.call-done = bf16[768,768]{1,0:T(8,128)(2,1)} async-done(((bf16[24,768]{1,0:T(8,128)(2,1)}), bf16[768,768]{1,0:T(8,128)(2,1)}) %all-gather.10.cloned.1.call-update) | async-done | bytes 1179664 | tf_op jit(solution)/shard_map/all_gather | solution.py:145
  73.1 50.5 %all-gather.14.cloned.1.call-done = bf16[768,768]{1,0:T(8,128)(2,1)} async-done(((bf16[24,768]{1,0:T(8,128)(2,1)}), bf16[768,768]{1,0:T(8,128)(2,1)}) %all-gather.14.cloned.1.call-update) | async-done | bytes 1179664 | tf_op jit(solution)/shard_map/all_gather | solution.py:146
  140.1 43.0 %all-gather.12.cloned.1.call-done = bf16[768,768]{1,0:T(8,128)(2,1)} async-done(((bf16[24,768]{1,0:T(8,128)(2,1)}), bf16[768,768]{1,0:T(8,128)(2,1)}) %all-gather.12.cloned.1.call-update) | async-done | bytes 1179664 | tf_op jit(solution)/shard_map/all_gather | solution.py:144
  191.0 30.1 %all-gather.24.cloned.1.call-done = bf16[1024,768]{1,0:T(8,128)(2,1)} async-done(((bf16[256,768]{1,0:T(8,128)(2,1)}), bf16[1024,768]{1,0:T(8,128)(2,1)}) %all-gather.24.cloned.1.call-update) | async-done | bytes 1572880 | tf_op jit(solution)/shard_map/all_gather | solution.py:163
  223.3 241.9 %while.60 = (s32[]{:T(128)}, f32[12,256]{1,0:T(8,128)S(1)}, f32[256,12,64]{0,2,1:T(8,128)}, s32[256]{0:T(256)}, s32[2]{0:T(128)}, /*index=5*/s32[1024]{0:T(1024)...) while((s32[]{:T(128)}, f32[12,256]{1,0:T(8,128)S(1)}, ...), condition=%wide.region_3.4_spmd.clone, body=%wide.region_1.3_spmd.clone.sunk | while | flops 414603776 | bytes 133137936 | solution.py:201
  289.4 48.3 %rev.42 = f32[12,256,512]{1,2,0:T(8,128)} reverse(f32[12,256,512]{1,2,0:T(8,128)} %copy.69), dimensions={2} | reverse | bytes 12582912 | tf_op jit(solution)/shard_map/while/body/eval_jaxpr/while/body/eval_jaxpr/rev | solution.py:62
  360.0 14.2 tile.39
  410.0 48.3 %rev.42 = f32[12,256,512]{1,2,0:T(8,128)} reverse(f32[12,256,512]{1,2,0:T(8,128)} %copy.69), dimensions={2} | reverse | bytes 12582912 | tf_op jit(solution)/shard_map/while/body/eval_jaxpr/while/body/eval_jaxpr/rev | solution.py:62
  495.3 349.3 %while.61 = (s32[]{:T(128)}, f32[256,12,64]{0,2,1:T(8,128)}, f32[12,32]{1,0:T(8,128)}, bf16[2,512,12,64]{1,3,2,0:T(8,128)(2,1)}, bf16[2,512,12,64]{1,3,2,0:T(8,1...) while((s32[]{:T(128)}, f32[256,12,64]{0,2,1:T(8,128)}, ...), condition=%wide.region_9.10_spmd.clone, body=%wide.region_7.9_spmd.clone.sunk | while | flops 1030591232 | bytes 274231168 | solution.py:291
  511.7 14.2 tile.41
  561.6 48.3 %rev.43 = f32[12,256,512]{1,2,0:T(8,128)} reverse(f32[12,256,512]{1,2,0:T(8,128)} %copy.71), dimensions={2} | reverse | bytes 12582912 | tf_op jit(solution)/shard_map/while/body/eval_jaxpr/while/body/eval_jaxpr/rev | solution.py:62
  637.3 20.8 %reshape.386 = f32[12,256,769]{2,1,0:T(8,128)} reshape(f32[12,196864]{1,0:T(8,128)} %pad_convert_fusion.2) | data formatting | bytes 18898944 | tf_op jit(solution)/shard_map/while/body/eval_jaxpr/while/body/eval_jaxpr/reshape | solution.py:78
  731.4 48.3 %rev.43 = f32[12,256,512]{1,2,0:T(8,128)} reverse(f32[12,256,512]{1,2,0:T(8,128)} %copy.71), dimensions={2} | reverse | bytes 12582912 | tf_op jit(solution)/shard_map/while/body/eval_jaxpr/while/body/eval_jaxpr/rev | solution.py:62
  807.4 20.8 %reshape.386 = f32[12,256,769]{2,1,0:T(8,128)} reshape(f32[12,196864]{1,0:T(8,128)} %pad_convert_fusion.2) | data formatting | bytes 18898944 | tf_op jit(solution)/shard_map/while/body/eval_jaxpr/while/body/eval_jaxpr/reshape | solution.py:78
  861.1 23.5 %reduce-scatter.12.cloned.1.call-done = bf16[1,256,768]{1,2,0:T(8,128)(2,1)} async-done(((bf16[1,1024,768]{1,2,0:T(8,128)(2,1)}), bf16[1,256,768]{1,2,0:T(8,128)(2,1)}) %reduce-scatter.12.cloned.1.call-update) | async-done | bytes 393232 | tf_op jit(solution)/shard_map/reduce_scatter | solution.py:314
  887.7 33.3 %reduce-scatter.10.cloned.1.call-done = bf16[1,256,768]{1,2,0:T(8,128)(2,1)} async-done(((bf16[1,1024,768]{1,2,0:T(8,128)(2,1)}), bf16[1,256,768]{1,2,0:T(8,128)(2,1)}) %reduce-scatter.10.cloned.1.call-update) | async-done | bytes 393232 | tf_op jit(solution)/shard_map/reduce_scatter | solution.py:311
  945.7 39.6 %all-reduce.2 = (f32[768]{0:T(1024)}, f32[768]{0:T(1024)}, f32[32,12]{0,1:T(8,128)}) all-reduce(f32[768]{0:T(1024)S(1)} %get-tuple-element.776, f32[768]{0:T(1024)S(1)} %copy-done.44, f32[32,12]{0,1:T(8,128)S(1)} %bitcast.268), channel_id=1, replica_groups=mesh['dp'=8,'seq'=4] {'dp','seq'}, use_global_device_ids=true, to_apply=%region_21.22 | all-reduce | flops 1920 | bytes 15360 | tf_op jit(solution)/shard_map/psum | solution.py:342
  986.4 38.5 %reduce-scatter.20.cloned.1.call-done = f32[24,768]{1,0:T(8,128)} async-done(((f32[768,768]{1,0:T(8,128)}), f32[24,768]{1,0:T(8,128)}) %reduce-scatter.20.cloned.1.call-update) | async-done | bytes 73744 | tf_op jit(solution)/shard_map/reduce_scatter | solution.py:336
  1024.9 104.7 %reduce-scatter.14.cloned.1.call-done = f32[24,768]{1,0:T(8,128)} async-done(((f32[768,768]{1,0:T(8,128)}), f32[24,768]{1,0:T(8,128)}) %reduce-scatter.14.cloned.1.call-update) | async-done | bytes 73744 | tf_op jit(solution)/shard_map/reduce_scatter | solution.py:333
  1129.6 103.9 %reduce-scatter.18.cloned.1.call-done = f32[24,768]{1,0:T(8,128)} async-done(((f32[768,768]{1,0:T(8,128)}), f32[24,768]{1,0:T(8,128)}) %reduce-scatter.18.cloned.1.call-update) | async-done | bytes 73744 | tf_op jit(solution)/shard_map/reduce_scatter | solution.py:335
  1233.5 104.7 %reduce-scatter.16.cloned.1.call-done = f32[24,768]{1,0:T(8,128)} async-done(((f32[768,768]{1,0:T(8,128)}), f32[24,768]{1,0:T(8,128)}) %reduce-scatter.16.cloned.1.call-update) | async-done | bytes 73744 | tf_op jit(solution)/shard_map/reduce_scatter | solution.py:334
  1338.2 119.4 %reduce-scatter.26.cloned.1.call-done = f32[64,768]{1,0:T(8,128)} async-done(((f32[2048,768]{1,0:T(8,128)}), f32[64,768]{1,0:T(8,128)}) %reduce-scatter.26.cloned.1.call-update) | async-done | bytes 196624 | tf_op jit(solution)/shard_map/reduce_scatter | solution.py:339
  1457.6 120.5 %reduce-scatter.24.cloned.1.call-done = f32[24,2048]{1,0:T(8,128)} async-done(((f32[768,2048]{1,0:T(8,128)}), f32[24,2048]{1,0:T(8,128)}) %reduce-scatter.24.cloned.1.call-update) | async-done | bytes 196624 | tf_op jit(solution)/shard_map/reduce_scatter | solution.py:338
  1578.1 119.7 %reduce-scatter.22.cloned.1.call-done = f32[24,2048]{1,0:T(8,128)} async-done(((f32[768,2048]{1,0:T(8,128)}), f32[24,2048]{1,0:T(8,128)}) %reduce-scatter.22.cloned.1.call-update) | async-done | bytes 196624 | tf_op jit(solution)/shard_map/reduce_scatter | solution.py:337
  (316 shorter events, 425.0 us)
Async XLA Ops:
  7.2 116.4 %copy-start.8 = (bf16[1,256,768]{2,1,0:T(8,128)(2,1)S(1)}, bf16[1,256,768]{2,1,0:T(8,128)(2,1)}, u32[]{:S(2)}) copy-start(bf16[1,256,768]{2,1,0:T(8,128)(2,1)} %param.18) | copy-start | bytes 1179652
  7.2 116.3 %copy-start.36 = (f32[768]{0:T(1024)S(1)}, f32[768]{0:T(1024)}, u32[]{:S(2)}) copy-start(f32[768]{0:T(1024)} %param.29) | copy-start | bytes 9220
  7.2 60.5 %all-gather.10.cloned.1.call-start = ((), (), s32[]{:S(2)}) async-start(), calls=%async_computation.9 | async-start | bytes 1216512 | tf_op jit(solution)/shard_map/all_gather | solution.py:145
  7.9 115.6 %all-gather.14.cloned.1.call-start = ((), (), s32[]{:S(2)}) async-start(), calls=%async_computation.11 | async-start | bytes 1216512 | tf_op jit(solution)/shard_map/all_gather | solution.py:146
  8.7 174.3 %all-gather.12.cloned.1.call-start = ((), (), s32[]{:S(2)}) async-start(), calls=%async_computation.10 | async-start | bytes 1216512 | tf_op jit(solution)/shard_map/all_gather | solution.py:144
  9.4 211.7 %all-gather.24.cloned.1.call-start = ((), (), s32[]{:S(2)}) async-start(), calls=%async_computation.25 | async-start | bytes 1966080 | tf_op jit(solution)/shard_map/all_gather | solution.py:163
  10.6 114.7 %copy-start.49 = (f32[256]{0:T(256)}, f32[256]{0:T(256)S(1)}, u32[]{:S(2)}) copy-start(f32[256]{0:T(256)S(1)} %fusion.50) | copy-start | bytes 3076
  10.6 172.4 %copy-start.42 = (f32[256]{0:T(256)}, f32[256]{0:T(256)S(1)}, u32[]{:S(2)}) copy-start(f32[256]{0:T(256)S(1)} %fusion.74) | copy-start | bytes 3076
  70.4 396.9 %all-gather.16.cloned.1.call-start = ((), (), s32[]{:S(2)}) async-start(), calls=%async_computation.12 | async-start | bytes 1216512 | tf_op jit(solution)/shard_map/all_gather | solution.py:147
  71.0 400.4 %all-gather.20.cloned.1.call-start = ((), (), s32[]{:S(2)}) async-start(), calls=%async_computation.14 | async-start | bytes 3244032 | tf_op jit(solution)/shard_map/all_gather | solution.py:149
  71.5 404.2 %all-gather.18.cloned.1.call-start = ((), (), s32[]{:S(2)}) async-start(), calls=%async_computation.13 | async-start | bytes 3244032 | tf_op jit(solution)/shard_map/all_gather | solution.py:148
  72.3 407.8 %all-gather.22.cloned.1.call-start = ((), (), s32[]{:S(2)}) async-start(), calls=%async_computation.15 | async-start | bytes 3244032 | tf_op jit(solution)/shard_map/all_gather | solution.py:150
  73.0 811.6 %reduce-scatter.12.cloned.1.call-start = ((), (), s32[]{:S(2)}) async-start(), calls=%async_computation.17 | async-start | bytes 1966080 | tf_op jit(solution)/shard_map/reduce_scatter | solution.py:314
  125.3 14.1 collective-permute-start
  127.2 57.8 %collective-permute-start.2 = (bf16[1,256,768]{2,1,0:T(8,128)(2,1)S(1)}, bf16[1,256,768]{2,1,0:T(8,128)(2,1)S(1)}, u32[]{:S(2)}, u32[]{:S(2)}) collective-permute-start(bf16[1,256,768]{2,1,0:T(8,128)(2,1)S(1)} %bitcast.261), channel_id=1, source_target_pairs={{1,0},{2,1},{3,2},{0,3},{5,4},{6,5},{7,6},{4,7},{9,8},{10,9},{11,1... | collective-permute-start | bytes 1179656 | tf_op jit(solution)/shard_map/ppermute | solution.py:26
  139.4 45.6 %collective-permute-start.1 = (bf16[1,256,768]{2,1,0:T(8,128)(2,1)S(1)}, bf16[1,256,768]{2,1,0:T(8,128)(2,1)S(1)}, u32[]{:S(2)}, u32[]{:S(2)}) collective-permute-start(bf16[1,256,768]{2,1,0:T(8,128)(2,1)S(1)} %collective-permute-done), channel_id=1, source_target_pairs={{0,1},{1,2},{2,3},{3,0},{4,5},{5,6},{6,7},{7,4},{8,9},{9,10},{10,1... | collective-permute-start | bytes 1179656 | tf_op jit(solution)/shard_map/ppermute | solution.py:24
  850.1 70.9 %reduce-scatter.10.cloned.1.call-start = ((), (), s32[]{:S(2)}) async-start(), calls=%async_computation.16 | async-start | bytes 1966080 | tf_op jit(solution)/shard_map/reduce_scatter | solution.py:311
  855.6 169.3 %reduce-scatter.20.cloned.1.call-start = ((), (), s32[]{:S(2)}) async-start(), calls=%async_computation.21 | async-start | bytes 2433024 | tf_op jit(solution)/shard_map/reduce_scatter | solution.py:336
  857.6 272.0 %reduce-scatter.14.cloned.1.call-start = ((), (), s32[]{:S(2)}) async-start(), calls=%async_computation.18 | async-start | bytes 2433024 | tf_op jit(solution)/shard_map/reduce_scatter | solution.py:333
  861.0 372.5 %reduce-scatter.18.cloned.1.call-start = ((), (), s32[]{:S(2)}) async-start(), calls=%async_computation.20 | async-start | bytes 2433024 | tf_op jit(solution)/shard_map/reduce_scatter | solution.py:335
  887.7 450.6 %reduce-scatter.16.cloned.1.call-start = ((), (), s32[]{:S(2)}) async-start(), calls=%async_computation.19 | async-start | bytes 2433024 | tf_op jit(solution)/shard_map/reduce_scatter | solution.py:334
  924.0 533.6 %reduce-scatter.26.cloned.1.call-start = ((), (), s32[]{:S(2)}) async-start(), calls=%async_computation.24 | async-start | bytes 6488064 | tf_op jit(solution)/shard_map/reduce_scatter | solution.py:339
  927.8 650.3 %reduce-scatter.24.cloned.1.call-start = ((), (), s32[]{:S(2)}) async-start(), calls=%async_computation.23 | async-start | bytes 6488064 | tf_op jit(solution)/shard_map/reduce_scatter | solution.py:338
  932.9 764.9 %reduce-scatter.22.cloned.1.call-start = ((), (), s32[]{:S(2)}) async-start(), calls=%async_computation.22 | async-start | bytes 6488064 | tf_op jit(solution)/shard_map/reduce_scatter | solution.py:337
  (65 other events, 623.9 us)
Sparse Core Ops, SparseCore 0:
  10.8 56.7 all-gather.9
  70.5 53.0 all-gather.13
  126.3 56.6 all-gather.11
  185.0 36.0 all-gather.23
  223.7 52.9 all-gather.15
  279.5 57.9 all-gather.19
  340.4 57.8 all-gather.17
  401.2 57.8 all-gather.21
  850.2 34.2 reduce-scatter.11
  886.7 34.2 reduce-scatter.9
  926.9 97.9 reduce-scatter.19
  1031.5 98.0 reduce-scatter.13
  1135.5 97.9 reduce-scatter.17
  1240.0 98.1 reduce-scatter.15
  1344.3 113.3 reduce-scatter.25
  1464.6 113.4 reduce-scatter.23
  1584.2 113.5 reduce-scatter.21
